TPU v7x, 32 devices: a whole 2x2x4 slice. The times are simulated.
32 devices in a mesh: group: 2 (over y), seq: 16 (over z, x, core).
Axes of the slice: x: 2, y: 2, z: 4, core: 2. Of those that a mesh axis runs over, the one named last changes fastest.
Arguments:
- queries: bfloat16 [4096, 4096], P(('group', 'seq')), parts along dimension 0, may hold values from -64 to 64
- key_vectors: bfloat16 [4096, 1024], P(('group', 'seq')), parts along dimension 0, may hold values from -2 to 2
- value_vectors: bfloat16 [4096, 1024], P(('group', 'seq')), parts along dimension 0, may hold values from -6 to 6
- grad_output: bfloat16 [4096, 4096], P(('group', 'seq')), parts along dimension 0, may hold values from -6 to 6
- document_ids: int32 [4096], P('group'), parts along dimension 0, may hold values from 0 to 3, never falling along the last dimension, each value on 1 to 1024 neighbouring positions
Outputs:
- attention_out: bfloat16 [4096, 4096], P(('group', 'seq')), parts along dimension 0
- grad_queries: bfloat16 [4096, 4096], P(('group', 'seq')), parts along dimension 0
- grad_keys: bfloat16 [4096, 1024], P(('group', 'seq')), parts along dimension 0
- grad_values: bfloat16 [4096, 1024], P(('group', 'seq')), parts along dimension 0
There are 2 independent parts, one for each index of `group`. A program takes and returns all parts, laid end to end along the dimension named above; each array names one. Nothing has to cross between parts.
Inputs may be any that keep to these rules, and one draw needn't show every extreme that they name: `document_ids`: document numbers never fall along positions; each document covers 1 to 1024 consecutive positions and one covers exactly 1024.
All inputs are finite; a program needn't handle non-finite values.
Results may differ from a plain program's by a relative error of at most 0.015.
Values may be sent and summed in bfloat16 or wider, within the bound.
No kernel may reach another device: no remote copies, remote signals or barrier semaphores. Data moves between devices by JAX's collectives and lax.ppermute only.
A program may use at most 128 MiB of HBM per device.

v0:
```python
import math
import jax
import jax.numpy as jnp
from jax import lax
from jax.sharding import PartitionSpec as P

H = 32
KV = 8
HD = 128
MOST = 1024


def shifted(block, axis, distance):
    devices = range(lax.axis_size(axis))
    route = [(i - distance, i) for i in devices if i - distance in devices]
    return lax.ppermute(block, axis, route)


def attend_block(query_block, grad_block, key_block, value_block, allowed):
    score_scale = 1.0 / math.sqrt(query_block.shape[-1])
    scores = (
        jnp.einsum("qgd,kd->gqk", query_block, key_block, preferred_element_type=jnp.float32)
        * score_scale
    )
    scores = jnp.where(allowed[None], scores, -1e30)
    row_max = jnp.max(scores, axis=-1, keepdims=True)
    weights = jnp.exp(scores - row_max)
    softmax = weights / jnp.sum(weights, axis=-1, keepdims=True)
    probs_low = softmax.astype(jnp.bfloat16)
    output = jnp.einsum(
        "gqk,kd->qgd", probs_low, value_block, preferred_element_type=jnp.float32
    ).astype(jnp.bfloat16)
    row_delta = jnp.sum(grad_block.astype(jnp.float32) * output.astype(jnp.float32), axis=-1)
    grad_probs = jnp.einsum(
        "qgd,kd->gqk", grad_block, value_block, preferred_element_type=jnp.float32
    )
    grad_scores = (softmax * (grad_probs - jnp.transpose(row_delta)[:, :, None])).astype(
        jnp.bfloat16
    )
    grad_query = (
        jnp.einsum("gqk,kd->qgd", grad_scores, key_block, preferred_element_type=jnp.float32)
        * score_scale
    ).astype(jnp.bfloat16)
    grad_key = (
        jnp.einsum("gqk,qgd->kd", grad_scores, query_block, preferred_element_type=jnp.float32)
        * score_scale
    )
    grad_value = jnp.einsum(
        "gqk,qgd->kd", probs_low, grad_block, preferred_element_type=jnp.float32
    )
    return (output, grad_query, grad_key, grad_value)


def on_device(queries, key_vectors, value_vectors, grad_output, document_ids):
    devices = lax.axis_size("seq")
    position = lax.axis_index("seq")
    local_rows = queries.shape[0]
    group = H // KV
    ratio = devices // KV
    slot_rows = local_rows // ratio
    block_len = slot_rows * devices
    block_rows = min(512, block_len)

    def to_slots(tensor, columns):
        return (
            tensor.reshape(ratio, slot_rows, KV, columns)
            .transpose(1, 2, 0, 3)
            .reshape(slot_rows, devices, columns)
        )

    def from_slots(tensor, columns):
        height = tensor.shape[0]
        return tensor.reshape(height, KV, ratio, columns).transpose(2, 0, 1, 3)

    query_send = to_slots(queries, group * HD)
    grad_send = to_slots(grad_output, group * HD)
    key_send = to_slots(key_vectors, HD)
    value_send = to_slots(value_vectors, HD)
    query_in, grad_in, key_in, value_in = (
        lax.all_to_all(query_send, "seq", split_axis=1, concat_axis=1, tiled=True),
        lax.all_to_all(grad_send, "seq", split_axis=1, concat_axis=1, tiled=True),
        lax.all_to_all(key_send, "seq", split_axis=1, concat_axis=1, tiled=True),
        lax.all_to_all(value_send, "seq", split_axis=1, concat_axis=1, tiled=True),
    )
    query_head = query_in.reshape(block_len, group, HD)
    grad_head = grad_in.reshape(block_len, group, HD)
    key_flat = key_in.reshape(-1, HD)
    value_flat = value_in.reshape(-1, HD)
    stacked = jnp.stack([key_flat, value_flat])
    previous = shifted(stacked, "seq", 1)
    key_window = jnp.concatenate([previous[0], key_flat], axis=0)
    value_window = jnp.concatenate([previous[1], value_flat], axis=0)
    start = position % ratio * block_len
    padded_ids = jnp.concatenate([jnp.full((MOST,), -1, jnp.int32), document_ids])
    column_ids_all = lax.dynamic_slice_in_dim(padded_ids, start, MOST + block_len)
    row_ids_all = lax.dynamic_slice_in_dim(document_ids, start, block_len)
    column_index = jnp.arange(block_rows + MOST, dtype=jnp.int32)[None, :]
    row_index = jnp.arange(block_rows, dtype=jnp.int32)[:, None]

    def one_block(step_index, totals):
        out_all, dq_all, key_grad, value_grad = totals
        offset = step_index * block_rows
        query_block = lax.dynamic_slice_in_dim(query_head, offset, block_rows, 0)
        grad_block = lax.dynamic_slice_in_dim(grad_head, offset, block_rows, 0)
        key_block = lax.dynamic_slice_in_dim(key_window, offset, block_rows + MOST, 0)
        value_block = lax.dynamic_slice_in_dim(value_window, offset, block_rows + MOST, 0)
        row_ids = lax.dynamic_slice_in_dim(row_ids_all, offset, block_rows)
        column_ids = lax.dynamic_slice_in_dim(column_ids_all, offset, block_rows + MOST)
        allowed = (row_ids[:, None] == column_ids[None, :]) & (column_index <= row_index + MOST)
        output, grad_query, grad_key, grad_value = attend_block(
            query_block, grad_block, key_block, value_block, allowed
        )
        out_all = lax.dynamic_update_slice_in_dim(out_all, output, offset, 0)
        dq_all = lax.dynamic_update_slice_in_dim(dq_all, grad_query, offset, 0)
        key_grad = lax.dynamic_update_slice_in_dim(
            key_grad,
            lax.dynamic_slice_in_dim(key_grad, offset, block_rows + MOST, 0) + grad_key,
            offset,
            0,
        )
        value_grad = lax.dynamic_update_slice_in_dim(
            value_grad,
            lax.dynamic_slice_in_dim(value_grad, offset, block_rows + MOST, 0) + grad_value,
            offset,
            0,
        )
        return (out_all, dq_all, key_grad, value_grad)

    initial = (
        jnp.zeros((block_len, group, HD), jnp.bfloat16),
        jnp.zeros((block_len, group, HD), jnp.bfloat16),
        jnp.zeros((MOST + block_len, HD), jnp.float32),
        jnp.zeros((MOST + block_len, HD), jnp.float32),
    )
    out_all, dq_all, key_grad, value_grad = lax.fori_loop(
        0, block_len // block_rows, one_block, initial
    )
    out_send = out_all.reshape(slot_rows, devices, group * HD)
    dq_send = dq_all.reshape(slot_rows, devices, group * HD)
    returned = shifted(
        jnp.stack([key_grad[:MOST], value_grad[:MOST]]).astype(jnp.bfloat16), "seq", -1
    ).astype(jnp.float32)
    key_own = key_grad[MOST:].at[block_len - MOST :].add(returned[0]).astype(jnp.bfloat16)
    value_own = value_grad[MOST:].at[block_len - MOST :].add(returned[1]).astype(jnp.bfloat16)
    out_back, dq_back, key_back, value_back = (
        lax.all_to_all(out_send, "seq", split_axis=1, concat_axis=1, tiled=True),
        lax.all_to_all(dq_send, "seq", split_axis=1, concat_axis=1, tiled=True),
        lax.all_to_all(
            key_own.reshape(slot_rows, devices, HD), "seq", split_axis=1, concat_axis=1, tiled=True
        ),
        lax.all_to_all(
            value_own.reshape(slot_rows, devices, HD),
            "seq",
            split_axis=1,
            concat_axis=1,
            tiled=True,
        ),
    )
    grad_keys = from_slots(key_back, HD).reshape(local_rows, KV * HD)
    grad_values = from_slots(value_back, HD).reshape(local_rows, KV * HD)
    attention_out = from_slots(out_back, group * HD).reshape(local_rows, H * HD)
    grad_queries = from_slots(dq_back, group * HD).reshape(local_rows, H * HD)
    return (attention_out, grad_queries, grad_keys, grad_values)


def solution(mesh):
    placed = (
        P(("group", "seq"), None),
        P(("group", "seq"), None),
        P(("group", "seq"), None),
        P(("group", "seq"), None),
        P("group"),
    )
    return jax.shard_map(
        on_device,
        mesh=mesh,
        in_specs=placed,
        out_specs=(
            P(("group", "seq"), None),
            P(("group", "seq"), None),
            P(("group", "seq"), None),
            P(("group", "seq"), None),
        ),
        check_vma=False,
    )
```

profile of v0, /device:TPU:11, one launch (start us, length us, event | category | flops | bytes accessed | tf_op | source)
XLA Modules:
  0.0 312.5 jit_solution(9346794623854736078)
XLA Ops:
  2.4 6.6 %all-to-all-start = ((bf16[64,16,128]{2,0,1:T(8,128)(2,1)}), bf16[64,16,128]{2,0,1:T(8,128)(2,1)S(1)}, u32[]{:S(2)}, u32[]{:S(2)}) async-start(bf16[64,16,128]{2,0,1:T(8,128)(2,1)} %bitcast.1), calls=%async_computation | async-start | bytes 524288 | tf_op jit(solution)/shard_map/all_to_all | solution.py:82
  10.7 6.2 %all-to-all-done = bf16[64,16,128]{2,0,1:T(8,128)(2,1)S(1)} async-done(((bf16[64,16,128]{2,0,1:T(8,128)(2,1)}), bf16[64,16,128]{2,0,1:T(8,128)(2,1)S(1)}, u32[]{:S(2)}, u32[]{:S(2)}) %all-to-all-start) | async-done | bytes 262176 | tf_op jit(solution)/shard_map/all_to_all | solution.py:82
  16.9 5.5 %all-to-all-start.1 = ((bf16[64,16,128]{2,0,1:T(8,128)(2,1)}), bf16[64,16,128]{2,0,1:T(8,128)(2,1)S(1)}, u32[]{:S(2)}, u32[]{:S(2)}) async-start(bf16[64,16,128]{2,0,1:T(8,128)(2,1)} %bitcast.4), calls=%async_computation.1 | async-start | bytes 524288 | tf_op jit(solution)/shard_map/all_to_all | solution.py:83
  25.4 5.0 %all-to-all-done.1 = bf16[64,16,128]{2,0,1:T(8,128)(2,1)S(1)} async-done(((bf16[64,16,128]{2,0,1:T(8,128)(2,1)}), bf16[64,16,128]{2,0,1:T(8,128)(2,1)S(1)}, u32[]{:S(2)}, u32[]{:S(2)}) %all-to-all-start.1) | async-done | bytes 262176 | tf_op jit(solution)/shard_map/all_to_all | solution.py:83
  30.4 5.7 %all-to-all-start.2 = ((bf16[64,16,512]{2,0,1:T(8,128)(2,1)}), bf16[64,16,512]{2,0,1:T(8,128)(2,1)S(1)}, u32[]{:S(2)}, u32[]{:S(2)}) async-start(bf16[64,16,512]{2,0,1:T(8,128)(2,1)} %bitcast.11), calls=%async_computation.2 | async-start | bytes 2097152 | tf_op jit(solution)/shard_map/all_to_all | solution.py:80
  39.1 21.9 %all-to-all-done.2 = bf16[64,16,512]{2,0,1:T(8,128)(2,1)S(1)} async-done(((bf16[64,16,512]{2,0,1:T(8,128)(2,1)}), bf16[64,16,512]{2,0,1:T(8,128)(2,1)S(1)}, u32[]{:S(2)}, u32[]{:S(2)}) %all-to-all-start.2) | async-done | bytes 1048608 | tf_op jit(solution)/shard_map/all_to_all | solution.py:80
  70.5 24.4 %collective-permute-done = bf16[2,1024,128]{2,1,0:T(8,128)(2,1)S(1)} collective-permute-done((bf16[2,1024,128]{2,1,0:T(8,128)(2,1)}, bf16[2,1024,128]{2,1,0:T(8,128)(2,1)S(1)}, u32[]{:S(2)}, u32[]{:S(2)}) %collective-permute-start) | collective-permute-done | bytes 524320 | tf_op jit(solution)/shard_map/ppermute | solution.py:16
  105.9 102.4 %while.24 = (s32[]{:T(128)}, bf16[1024,4,128]{2,1,0:T(4,128)(2,1)}, bf16[1024,4,128]{2,1,0:T(4,128)(2,1)}, f32[2048,128]{1,0:T(8,128)}, f32[2048,128]{1,0:T(8,12...) while((s32[]{:T(128)}, bf16[1024,4,128]{2,1,0:T(4,128)(2,1)}, ...), condition=%wide.region_4.5_spmd.clone, body=%wide.region_0.4_spmd.clone.sunk | while | flops 4874371072 | bytes 147394880 | solution.py:135
  110.7 10.0 %fusion.83 = (f32[4,512]{1,0:T(4,128)S(1)}, f32[4,512,1536]{1,2,0:T(8,128)}) fusion(f32[1536,512,4]{1,0,2:T(8,128)S(1)} %fusion.81, pred[512,1536]{0,1:T(8,128)(4,1)} %fusion.82), kind=kOutput, calls=%fused_computation.72.clone.1 | output fusion | flops 18875904 | bytes 25960448 | tf_op jit(solution)/shard_map/while/body/eval_jaxpr/sub | solution.py:27
  120.7 9.1 %fusion.84 = bf16[4,512,1536]{1,2,0:T(8,128)(2,1)} fusion(f32[4,512,1536]{1,2,0:T(8,128)} %get-tuple-element.452, f32[4,512]{1,0:T(4,128)S(1)} %get-tuple-element.453), kind=kLoop, calls=%fused_computation.13.clone.1 | loop fusion | flops 6291456 | bytes 18882560 | tf_op jit(solution)/shard_map/while/body/eval_jaxpr/convert_element_type | solution.py:29
  134.2 5.9 %fusion.85 = bf16[4,512,1536]{1,2,0:T(8,128)(2,1)S(1)} fusion(bf16[512,4,128]{0,2,1:T(8,128)(2,1)S(1)} %copy.153, f32[4,512]{1,0:T(4,128)S(1)} %bitcast.201, f32[4,512,1536]{1,2,0:T(8,128)} %get-tuple-element.452, f32[4,512]{1,0:T(4,128)S(1)} %get-tuple-element.453, bf16[2048,128]{1,0:T(8,128)(2,1)} %get-tuple-element.495, s32[]{:T(128)S(6)} %select_n.66), kind=kOutput, calls=%fused_computation.5.clone.1 | convolution fusion | flops 817889280 | bytes 19808260 | tf_op jit(solution)/shard_map/while/body/eval_jaxpr/qgd,kd->gqk/dot_general | solution.py:34
  145.8 5.6 %fusion.87 = f32[2048,128]{1,0:T(8,128)} fusion(f32[2048,128]{1,0:T(8,128)} %get-tuple-element.477, s32[]{:T(128)S(6)} %select_n.66, bf16[4,512,1536]{1,2,0:T(8,128)(2,1)} %copy-done, bf16[512,4,128]{2,1,0:T(4,128)(2,1)S(1)} %constant_dynamic-slice_fusion.5), kind=kOutput, calls=%fused_computation.20.clone.1 | convolution fusion | flops 805699584 | bytes 8388612 | tf_op jit(solution)/shard_map/while/body/eval_jaxpr/gqk,qgd->kd/dot_general | solution.py:45
  151.4 5.6 %fusion.88 = f32[2048,128]{1,0:T(8,128)} fusion(f32[2048,128]{1,0:T(8,128)} %get-tuple-element.478, s32[]{:T(128)S(6)} %select_n.66, bf16[4,512,1536]{1,2,0:T(8,128)(2,1)} %fusion.84, bf16[512,4,128]{0,2,1:T(8,128)(2,1)S(1)} %copy.153), kind=kOutput, calls=%fused_computation.22.clone.1 | convolution fusion | flops 805502976 | bytes 8388612 | tf_op jit(solution)/shard_map/while/body/eval_jaxpr/gqk,qgd->kd/dot_general | solution.py:48
  161.8 10.0 %fusion.83 = (f32[4,512]{1,0:T(4,128)S(1)}, f32[4,512,1536]{1,2,0:T(8,128)}) fusion(f32[1536,512,4]{1,0,2:T(8,128)S(1)} %fusion.81, pred[512,1536]{0,1:T(8,128)(4,1)} %fusion.82), kind=kOutput, calls=%fused_computation.72.clone.1 | output fusion | flops 18875904 | bytes 25960448 | tf_op jit(solution)/shard_map/while/body/eval_jaxpr/sub | solution.py:27
  171.8 9.1 %fusion.84 = bf16[4,512,1536]{1,2,0:T(8,128)(2,1)} fusion(f32[4,512,1536]{1,2,0:T(8,128)} %get-tuple-element.452, f32[4,512]{1,0:T(4,128)S(1)} %get-tuple-element.453), kind=kLoop, calls=%fused_computation.13.clone.1 | loop fusion | flops 6291456 | bytes 18882560 | tf_op jit(solution)/shard_map/while/body/eval_jaxpr/convert_element_type | solution.py:29
  185.4 5.9 %fusion.85 = bf16[4,512,1536]{1,2,0:T(8,128)(2,1)S(1)} fusion(bf16[512,4,128]{0,2,1:T(8,128)(2,1)S(1)} %copy.153, f32[4,512]{1,0:T(4,128)S(1)} %bitcast.201, f32[4,512,1536]{1,2,0:T(8,128)} %get-tuple-element.452, f32[4,512]{1,0:T(4,128)S(1)} %get-tuple-element.453, bf16[2048,128]{1,0:T(8,128)(2,1)} %get-tuple-element.495, s32[]{:T(128)S(6)} %select_n.66), kind=kOutput, calls=%fused_computation.5.clone.1 | convolution fusion | flops 817889280 | bytes 19808260 | tf_op jit(solution)/shard_map/while/body/eval_jaxpr/qgd,kd->gqk/dot_general | solution.py:34
  196.9 5.7 %fusion.87 = f32[2048,128]{1,0:T(8,128)} fusion(f32[2048,128]{1,0:T(8,128)} %get-tuple-element.477, s32[]{:T(128)S(6)} %select_n.66, bf16[4,512,1536]{1,2,0:T(8,128)(2,1)} %copy-done, bf16[512,4,128]{2,1,0:T(4,128)(2,1)S(1)} %constant_dynamic-slice_fusion.5), kind=kOutput, calls=%fused_computation.20.clone.1 | convolution fusion | flops 805699584 | bytes 8388612 | tf_op jit(solution)/shard_map/while/body/eval_jaxpr/gqk,qgd->kd/dot_general | solution.py:45
  202.6 5.7 %fusion.88 = f32[2048,128]{1,0:T(8,128)} fusion(f32[2048,128]{1,0:T(8,128)} %get-tuple-element.478, s32[]{:T(128)S(6)} %select_n.66, bf16[4,512,1536]{1,2,0:T(8,128)(2,1)} %fusion.84, bf16[512,4,128]{0,2,1:T(8,128)(2,1)S(1)} %copy.153), kind=kOutput, calls=%fused_computation.22.clone.1 | convolution fusion | flops 805502976 | bytes 8388612 | tf_op jit(solution)/shard_map/while/body/eval_jaxpr/gqk,qgd->kd/dot_general | solution.py:48
  212.5 10.1 %collective-permute-done.1 = bf16[2,1024,128]{2,1,0:T(8,128)(2,1)S(1)} collective-permute-done((bf16[2,1024,128]{2,1,0:T(8,128)(2,1)S(1)}, bf16[2,1024,128]{2,1,0:T(8,128)(2,1)S(1)}, u32[]{:S(2)}, u32[]{:S(2)}) %collective-permute-start.1) | collective-permute-done | bytes 524320 | tf_op jit(solution)/shard_map/ppermute | solution.py:16
  229.5 7.2 %all-to-all-done.7 = bf16[64,16,128]{2,0,1:T(8,128)(2,1)S(1)} async-done(((bf16[64,16,128]{2,0,1:T(8,128)(2,1)}), bf16[64,16,128]{2,0,1:T(8,128)(2,1)S(1)}, u32[]{:S(2)}, u32[]{:S(2)}) %all-to-all-start.7) | async-done | bytes 262176 | tf_op jit(solution)/shard_map/all_to_all | solution.py:151
  236.6 5.5 %all-to-all-start.6 = ((bf16[64,16,128]{2,0,1:T(8,128)(2,1)}), bf16[64,16,128]{2,0,1:T(8,128)(2,1)S(1)}, u32[]{:S(2)}, u32[]{:S(2)}) async-start(bf16[64,16,128]{2,0,1:T(8,128)(2,1)} %copy.111), calls=%async_computation.6 | async-start | bytes 524288 | tf_op jit(solution)/shard_map/all_to_all | solution.py:148
  250.2 5.7 %all-to-all-start.4 = ((bf16[64,16,512]{2,0,1:T(8,128)(2,1)}), bf16[64,16,512]{2,0,1:T(8,128)(2,1)S(1)}, u32[]{:S(2)}, u32[]{:S(2)}) async-start(bf16[64,16,512]{2,0,1:T(8,128)(2,1)} %copy.106), calls=%async_computation.4 | async-start | bytes 2097152 | tf_op jit(solution)/shard_map/all_to_all | solution.py:146
  257.9 22.9 %all-to-all-done.4 = bf16[64,16,512]{2,0,1:T(8,128)(2,1)S(1)} async-done(((bf16[64,16,512]{2,0,1:T(8,128)(2,1)}), bf16[64,16,512]{2,0,1:T(8,128)(2,1)S(1)}, u32[]{:S(2)}, u32[]{:S(2)}) %all-to-all-start.4) | async-done | bytes 1048608 | tf_op jit(solution)/shard_map/all_to_all | solution.py:146
  290.4 20.1 %all-to-all-done.5 = bf16[64,16,512]{2,0,1:T(8,128)(2,1)S(1)} async-done(((bf16[64,16,512]{2,0,1:T(8,128)(2,1)}), bf16[64,16,512]{2,0,1:T(8,128)(2,1)S(1)}, u32[]{:S(2)}, u32[]{:S(2)}) %all-to-all-start.5) | async-done | bytes 1048608 | tf_op jit(solution)/shard_map/all_to_all | solution.py:147
  (92 shorter events, 92.3 us)
Async XLA Ops:
  0.6 69.9 %copy-start.4 = (s32[2048]{0:T(1024)S(1)}, s32[2048]{0:T(1024)}, u32[]{:S(2)}) copy-start(s32[2048]{0:T(1024)} %param.19) | copy-start | bytes 24580
  2.4 14.5 %all-to-all-start = ((bf16[64,16,128]{2,0,1:T(8,128)(2,1)}), bf16[64,16,128]{2,0,1:T(8,128)(2,1)S(1)}, u32[]{:S(2)}, u32[]{:S(2)}) async-start(bf16[64,16,128]{2,0,1:T(8,128)(2,1)} %bitcast.1), calls=%async_computation | async-start | bytes 524288 | tf_op jit(solution)/shard_map/all_to_all | solution.py:82
  16.9 13.5 %all-to-all-start.1 = ((bf16[64,16,128]{2,0,1:T(8,128)(2,1)}), bf16[64,16,128]{2,0,1:T(8,128)(2,1)S(1)}, u32[]{:S(2)}, u32[]{:S(2)}) async-start(bf16[64,16,128]{2,0,1:T(8,128)(2,1)} %bitcast.4), calls=%async_computation.1 | async-start | bytes 524288 | tf_op jit(solution)/shard_map/all_to_all | solution.py:83
  30.4 30.6 %all-to-all-start.2 = ((bf16[64,16,512]{2,0,1:T(8,128)(2,1)}), bf16[64,16,512]{2,0,1:T(8,128)(2,1)S(1)}, u32[]{:S(2)}, u32[]{:S(2)}) async-start(bf16[64,16,512]{2,0,1:T(8,128)(2,1)} %bitcast.11), calls=%async_computation.2 | async-start | bytes 2097152 | tf_op jit(solution)/shard_map/all_to_all | solution.py:80
  61.0 38.6 %all-to-all-start.3 = ((bf16[64,16,512]{2,0,1:T(8,128)(2,1)}), bf16[64,16,512]{2,0,1:T(8,128)(2,1)S(1)}, u32[]{:S(2)}, u32[]{:S(2)}) async-start(bf16[64,16,512]{2,0,1:T(8,128)(2,1)} %bitcast.13), calls=%async_computation.3 | async-start | bytes 2097152 | tf_op jit(solution)/shard_map/all_to_all | solution.py:81
  67.1 27.8 %collective-permute-start = (bf16[2,1024,128]{2,1,0:T(8,128)(2,1)}, bf16[2,1024,128]{2,1,0:T(8,128)(2,1)S(1)}, u32[]{:S(2)}, u32[]{:S(2)}) collective-permute-start(bf16[2,1024,128]{2,1,0:T(8,128)(2,1)} %pad_maximum_fusion), channel_id=1, source_target_pairs={{0,1},{1,2},{2,3},{3,4},{4,5},{5,6},{6,7},{7,8},{8,9},{9,10},{10,1... | collective-permute-start | bytes 1572872 | tf_op jit(solution)/shard_map/ppermute | solution.py:16
  70.5 35.4 %dynamic-slice-start = ((s32[2048]{0:T(1024)}, s32[]{:T(128)}), s32[1024]{0:T(1024)S(1)}, s32[]{:S(2)}) async-start(s32[2048]{0:T(1024)} %param.19, s32[]{:T(128)} %select_n.46), calls=%async_computation.8 | async-start | bytes 8704 | tf_op jit(solution)/shard_map/dynamic_slice | solution.py:96
  120.7 9.1 %copy-start.1 = (bf16[1024,4,128]{2,1,0:T(4,128)(2,1)S(1)}, bf16[1024,4,128]{2,1,0:T(4,128)(2,1)}, u32[]{:S(2)}) copy-start(bf16[1024,4,128]{2,1,0:T(4,128)(2,1)} %get-tuple-element.500) | copy-start | bytes 3145732 | tf_op jit(solution)/shard_map/while
  140.1 2.7 copy-start
  171.8 9.1 %copy-start.1 = (bf16[1024,4,128]{2,1,0:T(4,128)(2,1)S(1)}, bf16[1024,4,128]{2,1,0:T(4,128)(2,1)}, u32[]{:S(2)}) copy-start(bf16[1024,4,128]{2,1,0:T(4,128)(2,1)} %get-tuple-element.500) | copy-start | bytes 3145732 | tf_op jit(solution)/shard_map/while
  191.3 2.7 copy-start
  208.2 47.6 %copy-start.2 = (bf16[1024,4,128]{2,1,0:T(4,128)(2,1)S(1)}, bf16[1024,4,128]{2,1,0:T(4,128)(2,1)}, u32[]{:S(2)}) copy-start(bf16[1024,4,128]{2,1,0:T(4,128)(2,1)} %get-tuple-element.262) | copy-start | bytes 3145732
  210.5 12.0 %collective-permute-start.1 = (bf16[2,1024,128]{2,1,0:T(8,128)(2,1)S(1)}, bf16[2,1024,128]{2,1,0:T(8,128)(2,1)S(1)}, u32[]{:S(2)}, u32[]{:S(2)}) collective-permute-start(bf16[2,1024,128]{2,1,0:T(8,128)(2,1)S(1)} %pad_maximum_fusion.3), channel_id=1, source_target_pairs={{1,0},{2,1},{3,2},{4,3},{5,4},{6,5},{7,6},{8,7},{9,8},{10,9},{11,1... | collective-permute-start | bytes 1572872 | tf_op jit(solution)/shard_map/ppermute | solution.py:16
  224.7 11.9 %all-to-all-start.7 = ((bf16[64,16,128]{2,0,1:T(8,128)(2,1)}), bf16[64,16,128]{2,0,1:T(8,128)(2,1)S(1)}, u32[]{:S(2)}, u32[]{:S(2)}) async-start(bf16[64,16,128]{2,0,1:T(8,128)(2,1)} %copy.113), calls=%async_computation.7 | async-start | bytes 524288 | tf_op jit(solution)/shard_map/all_to_all | solution.py:151
  236.6 13.5 %all-to-all-start.6 = ((bf16[64,16,128]{2,0,1:T(8,128)(2,1)}), bf16[64,16,128]{2,0,1:T(8,128)(2,1)S(1)}, u32[]{:S(2)}, u32[]{:S(2)}) async-start(bf16[64,16,128]{2,0,1:T(8,128)(2,1)} %copy.111), calls=%async_computation.6 | async-start | bytes 524288 | tf_op jit(solution)/shard_map/all_to_all | solution.py:148
  250.2 5.7 %copy-start.3 = (bf16[64,16,128]{2,0,1:T(8,128)(2,1)}, bf16[64,16,128]{2,0,1:T(8,128)(2,1)S(1)}, u32[]{:S(2)}) copy-start(bf16[64,16,128]{2,0,1:T(8,128)(2,1)S(1)} %all-to-all-done.6) | copy-start | bytes 786436
  250.2 30.6 %all-to-all-start.4 = ((bf16[64,16,512]{2,0,1:T(8,128)(2,1)}), bf16[64,16,512]{2,0,1:T(8,128)(2,1)S(1)}, u32[]{:S(2)}, u32[]{:S(2)}) async-start(bf16[64,16,512]{2,0,1:T(8,128)(2,1)} %copy.106), calls=%async_computation.4 | async-start | bytes 2097152 | tf_op jit(solution)/shard_map/all_to_all | solution.py:146
  280.8 29.8 %all-to-all-start.5 = ((bf16[64,16,512]{2,0,1:T(8,128)(2,1)}), bf16[64,16,512]{2,0,1:T(8,128)(2,1)S(1)}, u32[]{:S(2)}, u32[]{:S(2)}) async-start(bf16[64,16,512]{2,0,1:T(8,128)(2,1)} %copy.109), calls=%async_computation.5 | async-start | bytes 2097152 | tf_op jit(solution)/shard_map/all_to_all | solution.py:147
where the time goes:
time: 314 us; the launch traced here: 312 us
  waiting for transfers between devices  123 us (39%)
  local copies, waits for them, and re-layouts  48.3 us (15%)
  starting transfers between devices  48.1 us (15%)
  matrix products  47.9 us (15%)
  other arithmetic  44.5 us (14%)
    ppermute x2, waiting for transfers between devices, shifted(): return lax.ppermute(block, axis, route)  34.5 us
    all_to_all x1, waiting for transfers between devices, on_device(): lax.all_to_all(out_send, 'seq', split_axis=1, concat_axis=1, tiled=True)  22.9 us
    all_to_all x1, waiting for transfers between devices, on_device(): lax.all_to_all(query_send, 'seq', split_axis=1, concat_axis=1, tiled=True)  21.9 us
    all_to_all x1, waiting for transfers between devices, on_device(): lax.all_to_all(dq_send, 'seq', split_axis=1, concat_axis=1, tiled=True)  20.1 us
    sub x2, other arithmetic, attend_block(): weights = jnp.exp(scores - row_max)  20 us
    convert_element_type x2, other arithmetic, attend_block(): probs_low = softmax.astype(jnp.bfloat16)  18.2 us
    dot_general x2, matrix products, attend_block(): jnp.einsum('qgd,kd->gqk', grad_block, value_block, preferred_element_type...  11.7 us
    dot_general x2, matrix products, attend_block(): jnp.einsum('gqk,qgd->kd', probs_low, grad_block, preferred_element_type=j...  11.3 us
  transfers between devices with their start and end apart: 10, of which 9 were waited for; matrix products, arithmetic and copies ran while one was open for 8% of the time, Pallas kernels for 0%

commit v1 on v0

--- a/solution.py
+++ b/solution.py
@@ -8,6 +8,28 @@
 KV = 8
 HD = 128
 MOST = 1024
+
+
+def cut_along(value, dim, size):
+    before, after = (value.shape[:dim], value.shape[dim + 1 :])
+    return jnp.moveaxis(value.reshape(*before, size, -1, *after), dim, 0)
+
+
+def in_order(blocks, dim):
+    shape = list(blocks.shape[1:])
+    shape[dim] *= blocks.shape[0]
+    return jnp.moveaxis(blocks, 0, dim).reshape(shape)
+
+
+def swapped_with_each(shard, axis, split_dim, concat_dim):
+    peers, place = (lax.axis_size(axis), lax.axis_index(axis))
+    blocks = cut_along(shard, split_dim, peers)
+    finished = [blocks[place]]
+    for step in range(1, peers):
+        sent = blocks[place ^ step]
+        finished.append(lax.ppermute(sent, axis, [(i, i ^ step) for i in range(peers)]))
+    blocks = jnp.stack(finished)[place ^ jnp.arange(peers)]
+    return in_order(blocks, concat_dim)
 
 
 def shifted(block, axis, distance):
@@ -148,13 +170,7 @@
         lax.all_to_all(
             key_own.reshape(slot_rows, devices, HD), "seq", split_axis=1, concat_axis=1, tiled=True
         ),
-        lax.all_to_all(
-            value_own.reshape(slot_rows, devices, HD),
-            "seq",
-            split_axis=1,
-            concat_axis=1,
-            tiled=True,
-        ),
+        swapped_with_each(value_own.reshape(slot_rows, devices, HD), "seq", 1, 1),
     )
     grad_keys = from_slots(key_back, HD).reshape(local_rows, KV * HD)
     grad_values = from_slots(value_back, HD).reshape(local_rows, KV * HD)

time: 314 us -> 310 us (0.987)
  waiting for transfers between devices: 123 us -> 105 us
  starting transfers between devices: 48.1 us -> 60.3 us
    ppermute x0 -> x15, waiting for transfers between devices: none -> 29.9 us  [swapped_with_each(): lax.ppermute(sent, axis, [(i, i ^ step) for i in range(peers)])]
    all_to_all x1, waiting for transfers between devices: 22.9 us -> 0.01 us  [on_device(): lax.all_to_all(out_send, 'seq', split_axis=1, concat_axis=1, tiled=True)]
    ppermute x0 -> x15, starting transfers between devices: none -> 18.4 us  [swapped_with_each(): lax.ppermute(sent, axis, [(i, i ^ step) for i in range(peers)])]
    all_to_all x1, waiting for transfers between devices: 20.1 us -> 3.01 us  [on_device(): lax.all_to_all(dq_send, 'seq', split_axis=1, concat_axis=1, tiled=True)]
    all_to_all x1 -> x0, waiting for transfers between devices: 7.18 us -> none  [on_device(): lax.all_to_all(value_own.reshape(slot_rows, devices, HD), 'seq', split_ax...]
    all_to_all x1 -> x0, starting transfers between devices: 3.97 us -> none  [on_device(): lax.all_to_all(value_own.reshape(slot_rows, devices, HD), 'seq', split_ax...]
    unnamed x14 -> x44, local copies, waits for them, and re-layouts: 9.46 us -> 9.65 us
  transfers between devices with their start and end apart: 10 -> 24, of which waited for: 9 -> 11; matrix products, arithmetic and copies ran while one was open for 8% -> 8% of each run, Pallas kernels for 0% -> 0%
where the time goes in v1:
time: 310 us; the launch traced here: 308 us
  waiting for transfers between devices  105 us (34%)
  starting transfers between devices  60.3 us (19%)
  local copies, waits for them, and re-layouts  49.1 us (16%)
  matrix products  47.9 us (15%)
  other arithmetic  44.5 us (14%)
    ppermute x2, waiting for transfers between devices, shifted(): return lax.ppermute(block, axis, route)  34.5 us
    ppermute x15, waiting for transfers between devices, swapped_with_each(): lax.ppermute(sent, axis, [(i, i ^ step) for i in range(peers)])  29.9 us
    all_to_all x1, waiting for transfers between devices, on_device(): lax.all_to_all(query_send, 'seq', split_axis=1, concat_axis=1, tiled=True)  21.9 us
    sub x2, other arithmetic, attend_block(): weights = jnp.exp(scores - row_max)  19.9 us
    ppermute x15, starting transfers between devices, swapped_with_each(): lax.ppermute(sent, axis, [(i, i ^ step) for i in range(peers)])  18.4 us
    convert_element_type x2, other arithmetic, attend_block(): probs_low = softmax.astype(jnp.bfloat16)  18.2 us
    dot_general x2, matrix products, attend_block(): jnp.einsum('qgd,kd->gqk', grad_block, value_block, preferred_element_type...  11.7 us
    dot_general x2, matrix products, attend_block(): jnp.einsum('gqk,qgd->kd', grad_scores, query_block, preferred_element_typ...  11.3 us
  transfers between devices with their start and end apart: 24, of which 11 were waited for; matrix products, arithmetic and copies ran while one was open for 8% of the time, Pallas kernels for 0%

profile of v1, /device:TPU:11, one launch (start us, length us, event | category | flops | bytes accessed | tf_op | source)
XLA Modules:
  0.0 308.3 jit_solution(15068652751649944935)
XLA Ops:
  2.4 6.6 %all-to-all-start = ((bf16[64,16,128]{2,0,1:T(8,128)(2,1)}), bf16[64,16,128]{2,0,1:T(8,128)(2,1)S(1)}, u32[]{:S(2)}, u32[]{:S(2)}) async-start(bf16[64,16,128]{2,0,1:T(8,128)(2,1)} %bitcast.1), calls=%async_computation | async-start | bytes 524288 | tf_op jit(solution)/shard_map/all_to_all | solution.py:104
  10.7 6.2 %all-to-all-done = bf16[64,16,128]{2,0,1:T(8,128)(2,1)S(1)} async-done(((bf16[64,16,128]{2,0,1:T(8,128)(2,1)}), bf16[64,16,128]{2,0,1:T(8,128)(2,1)S(1)}, u32[]{:S(2)}, u32[]{:S(2)}) %all-to-all-start) | async-done | bytes 262176 | tf_op jit(solution)/shard_map/all_to_all | solution.py:104
  16.9 5.5 %all-to-all-start.1 = ((bf16[64,16,128]{2,0,1:T(8,128)(2,1)}), bf16[64,16,128]{2,0,1:T(8,128)(2,1)S(1)}, u32[]{:S(2)}, u32[]{:S(2)}) async-start(bf16[64,16,128]{2,0,1:T(8,128)(2,1)} %bitcast.4), calls=%async_computation.1 | async-start | bytes 524288 | tf_op jit(solution)/shard_map/all_to_all | solution.py:105
  25.4 5.0 %all-to-all-done.1 = bf16[64,16,128]{2,0,1:T(8,128)(2,1)S(1)} async-done(((bf16[64,16,128]{2,0,1:T(8,128)(2,1)}), bf16[64,16,128]{2,0,1:T(8,128)(2,1)S(1)}, u32[]{:S(2)}, u32[]{:S(2)}) %all-to-all-start.1) | async-done | bytes 262176 | tf_op jit(solution)/shard_map/all_to_all | solution.py:105
  30.4 5.7 %all-to-all-start.2 = ((bf16[64,16,512]{2,0,1:T(8,128)(2,1)}), bf16[64,16,512]{2,0,1:T(8,128)(2,1)S(1)}, u32[]{:S(2)}, u32[]{:S(2)}) async-start(bf16[64,16,512]{2,0,1:T(8,128)(2,1)} %bitcast.11), calls=%async_computation.2 | async-start | bytes 2097152 | tf_op jit(solution)/shard_map/all_to_all | solution.py:102
  39.1 21.9 %all-to-all-done.2 = bf16[64,16,512]{2,0,1:T(8,128)(2,1)S(1)} async-done(((bf16[64,16,512]{2,0,1:T(8,128)(2,1)}), bf16[64,16,512]{2,0,1:T(8,128)(2,1)S(1)}, u32[]{:S(2)}, u32[]{:S(2)}) %all-to-all-start.2) | async-done | bytes 1048608 | tf_op jit(solution)/shard_map/all_to_all | solution.py:102
  61.0 4.9 %all-to-all-start.3 = ((bf16[64,16,512]{2,0,1:T(8,128)(2,1)}), bf16[64,16,512]{2,0,1:T(8,128)(2,1)S(1)}, u32[]{:S(2)}, u32[]{:S(2)}) async-start(bf16[64,16,512]{2,0,1:T(8,128)(2,1)} %bitcast.13), calls=%async_computation.3 | async-start | bytes 2097152 | tf_op jit(solution)/shard_map/all_to_all | solution.py:103
  70.5 24.4 %collective-permute-done = bf16[2,1024,128]{2,1,0:T(8,128)(2,1)S(1)} collective-permute-done((bf16[2,1024,128]{2,1,0:T(8,128)(2,1)}, bf16[2,1024,128]{2,1,0:T(8,128)(2,1)S(1)}, u32[]{:S(2)}, u32[]{:S(2)}) %collective-permute-start) | collective-permute-done | bytes 524320 | tf_op jit(solution)/shard_map/ppermute | solution.py:38
  106.0 102.3 %while.24 = (s32[]{:T(128)}, bf16[1024,4,128]{2,1,0:T(4,128)(2,1)}, bf16[1024,4,128]{2,1,0:T(4,128)(2,1)}, f32[2048,128]{1,0:T(8,128)}, f32[2048,128]{1,0:T(8,12...) while((s32[]{:T(128)}, bf16[1024,4,128]{2,1,0:T(4,128)(2,1)}, ...), condition=%wide.region_4.5_spmd.clone, body=%wide.region_0.4_spmd.clone.sunk | while | flops 4874371072 | bytes 147394880 | solution.py:157
  110.8 10.0 %fusion.84 = (f32[4,512]{1,0:T(4,128)S(1)}, f32[4,512,1536]{1,2,0:T(8,128)}) fusion(f32[1536,512,4]{1,0,2:T(8,128)S(1)} %fusion.82, pred[512,1536]{0,1:T(8,128)(4,1)} %fusion.83), kind=kOutput, calls=%fused_computation.123.clone.1 | output fusion | flops 18875904 | bytes 25960448 | tf_op jit(solution)/shard_map/while/body/eval_jaxpr/sub | solution.py:49
  120.7 9.1 %fusion.85 = bf16[4,512,1536]{1,2,0:T(8,128)(2,1)} fusion(f32[4,512,1536]{1,2,0:T(8,128)} %get-tuple-element.468, f32[4,512]{1,0:T(4,128)S(1)} %get-tuple-element.469), kind=kLoop, calls=%fused_computation.14.clone.1 | loop fusion | flops 6291456 | bytes 18882560 | tf_op jit(solution)/shard_map/while/body/eval_jaxpr/convert_element_type | solution.py:51
  134.3 5.9 %fusion.86 = bf16[4,512,1536]{1,2,0:T(8,128)(2,1)S(1)} fusion(bf16[512,4,128]{0,2,1:T(8,128)(2,1)S(1)} %copy.197, f32[4,512]{1,0:T(4,128)S(1)} %bitcast.286, f32[4,512,1536]{1,2,0:T(8,128)} %get-tuple-element.468, f32[4,512]{1,0:T(4,128)S(1)} %get-tuple-element.469, bf16[2048,128]{1,0:T(8,128)(2,1)} %get-tuple-element.511, s32[]{:T(128)S(6)} %select_n.144), kind=kOutput, calls=%fused_computation.6.clone.1 | convolution fusion | flops 817889280 | bytes 19808260 | tf_op jit(solution)/shard_map/while/body/eval_jaxpr/qgd,kd->gqk/dot_general | solution.py:56
  145.8 5.7 %fusion.88 = f32[2048,128]{1,0:T(8,128)} fusion(f32[2048,128]{1,0:T(8,128)} %get-tuple-element.493, s32[]{:T(128)S(6)} %select_n.144, bf16[4,512,1536]{1,2,0:T(8,128)(2,1)} %copy-done, bf16[512,4,128]{2,1,0:T(4,128)(2,1)S(1)} %constant_dynamic-slice_fusion.21), kind=kOutput, calls=%fused_computation.21.clone.1 | convolution fusion | flops 805699584 | bytes 8388612 | tf_op jit(solution)/shard_map/while/body/eval_jaxpr/gqk,qgd->kd/dot_general | solution.py:67
  151.5 5.6 %fusion.89 = f32[2048,128]{1,0:T(8,128)} fusion(f32[2048,128]{1,0:T(8,128)} %get-tuple-element.494, s32[]{:T(128)S(6)} %select_n.144, bf16[4,512,1536]{1,2,0:T(8,128)(2,1)} %fusion.85, bf16[512,4,128]{0,2,1:T(8,128)(2,1)S(1)} %copy.197), kind=kOutput, calls=%fused_computation.23.clone.1 | convolution fusion | flops 805502976 | bytes 8388612 | tf_op jit(solution)/shard_map/while/body/eval_jaxpr/gqk,qgd->kd/dot_general | solution.py:70
  161.9 10.0 %fusion.84 = (f32[4,512]{1,0:T(4,128)S(1)}, f32[4,512,1536]{1,2,0:T(8,128)}) fusion(f32[1536,512,4]{1,0,2:T(8,128)S(1)} %fusion.82, pred[512,1536]{0,1:T(8,128)(4,1)} %fusion.83), kind=kOutput, calls=%fused_computation.123.clone.1 | output fusion | flops 18875904 | bytes 25960448 | tf_op jit(solution)/shard_map/while/body/eval_jaxpr/sub | solution.py:49
  171.8 9.1 %fusion.85 = bf16[4,512,1536]{1,2,0:T(8,128)(2,1)} fusion(f32[4,512,1536]{1,2,0:T(8,128)} %get-tuple-element.468, f32[4,512]{1,0:T(4,128)S(1)} %get-tuple-element.469), kind=kLoop, calls=%fused_computation.14.clone.1 | loop fusion | flops 6291456 | bytes 18882560 | tf_op jit(solution)/shard_map/while/body/eval_jaxpr/convert_element_type | solution.py:51
  185.4 5.9 %fusion.86 = bf16[4,512,1536]{1,2,0:T(8,128)(2,1)S(1)} fusion(bf16[512,4,128]{0,2,1:T(8,128)(2,1)S(1)} %copy.197, f32[4,512]{1,0:T(4,128)S(1)} %bitcast.286, f32[4,512,1536]{1,2,0:T(8,128)} %get-tuple-element.468, f32[4,512]{1,0:T(4,128)S(1)} %get-tuple-element.469, bf16[2048,128]{1,0:T(8,128)(2,1)} %get-tuple-element.511, s32[]{:T(128)S(6)} %select_n.144), kind=kOutput, calls=%fused_computation.6.clone.1 | convolution fusion | flops 817889280 | bytes 19808260 | tf_op jit(solution)/shard_map/while/body/eval_jaxpr/qgd,kd->gqk/dot_general | solution.py:56
  196.9 5.6 %fusion.88 = f32[2048,128]{1,0:T(8,128)} fusion(f32[2048,128]{1,0:T(8,128)} %get-tuple-element.493, s32[]{:T(128)S(6)} %select_n.144, bf16[4,512,1536]{1,2,0:T(8,128)(2,1)} %copy-done, bf16[512,4,128]{2,1,0:T(4,128)(2,1)S(1)} %constant_dynamic-slice_fusion.21), kind=kOutput, calls=%fused_computation.21.clone.1 | convolution fusion | flops 805699584 | bytes 8388612 | tf_op jit(solution)/shard_map/while/body/eval_jaxpr/gqk,qgd->kd/dot_general | solution.py:67
  202.6 5.6 %fusion.89 = f32[2048,128]{1,0:T(8,128)} fusion(f32[2048,128]{1,0:T(8,128)} %get-tuple-element.494, s32[]{:T(128)S(6)} %select_n.144, bf16[4,512,1536]{1,2,0:T(8,128)(2,1)} %fusion.85, bf16[512,4,128]{0,2,1:T(8,128)(2,1)S(1)} %copy.197), kind=kOutput, calls=%fused_computation.23.clone.1 | convolution fusion | flops 805502976 | bytes 8388612 | tf_op jit(solution)/shard_map/while/body/eval_jaxpr/gqk,qgd->kd/dot_general | solution.py:70
  212.5 10.1 %collective-permute-done.1 = bf16[2,1024,128]{2,1,0:T(8,128)(2,1)S(1)} collective-permute-done((bf16[2,1024,128]{2,1,0:T(8,128)(2,1)S(1)}, bf16[2,1024,128]{2,1,0:T(8,128)(2,1)S(1)}, u32[]{:S(2)}, u32[]{:S(2)}) %collective-permute-start.1) | collective-permute-done | bytes 524320 | tf_op jit(solution)/shard_map/ppermute | solution.py:38
  231.7 4.9 %all-to-all-done.6 = bf16[64,16,128]{2,0,1:T(8,128)(2,1)S(1)} async-done(((bf16[64,16,128]{2,0,1:T(8,128)(2,1)}), bf16[64,16,128]{2,0,1:T(8,128)(2,1)S(1)}, u32[]{:S(2)}, u32[]{:S(2)}) %all-to-all-start.6) | async-done | bytes 262176 | tf_op jit(solution)/shard_map/all_to_all | solution.py:170
  236.6 5.7 %all-to-all-start.5 = ((bf16[64,16,512]{2,0,1:T(8,128)(2,1)}), bf16[64,16,512]{2,0,1:T(8,128)(2,1)S(1)}, u32[]{:S(2)}, u32[]{:S(2)}) async-start(bf16[64,16,512]{2,0,1:T(8,128)(2,1)} %copy.107), calls=%async_computation.5 | async-start | bytes 2097152 | tf_op jit(solution)/shard_map/all_to_all | solution.py:169
  254.2 6.6 %collective-permute-done.5 = bf16[64,1,128]{2,0,1:T(8,128)(2,1)S(1)} collective-permute-done((bf16[64,1,128]{2,0,1:T(8,128)(2,1)S(1)}, bf16[64,1,128]{2,0,1:T(8,128)(2,1)S(1)}, u32[]{:S(2)}, u32[]{:S(2)}) %collective-permute-start.5) | collective-permute-done | bytes 16416 | tf_op jit(solution)/shard_map/ppermute | solution.py:30
  277.8 21.6 %collective-permute-done.13 = bf16[64,1,128]{2,0,1:T(8,128)(2,1)S(1)} collective-permute-done((bf16[64,1,128]{2,0,1:T(8,128)(2,1)S(1)}, bf16[64,1,128]{2,0,1:T(8,128)(2,1)S(1)}, u32[]{:S(2)}, u32[]{:S(2)}) %collective-permute-start.13) | collective-permute-done | bytes 16416 | tf_op jit(solution)/shard_map/ppermute | solution.py:30
  (154 shorter events, 105.6 us)
Async XLA Ops:
  2.4 14.5 %all-to-all-start = ((bf16[64,16,128]{2,0,1:T(8,128)(2,1)}), bf16[64,16,128]{2,0,1:T(8,128)(2,1)S(1)}, u32[]{:S(2)}, u32[]{:S(2)}) async-start(bf16[64,16,128]{2,0,1:T(8,128)(2,1)} %bitcast.1), calls=%async_computation | async-start | bytes 524288 | tf_op jit(solution)/shard_map/all_to_all | solution.py:104
  16.9 13.5 %all-to-all-start.1 = ((bf16[64,16,128]{2,0,1:T(8,128)(2,1)}), bf16[64,16,128]{2,0,1:T(8,128)(2,1)S(1)}, u32[]{:S(2)}, u32[]{:S(2)}) async-start(bf16[64,16,128]{2,0,1:T(8,128)(2,1)} %bitcast.4), calls=%async_computation.1 | async-start | bytes 524288 | tf_op jit(solution)/shard_map/all_to_all | solution.py:105
  30.4 30.6 %all-to-all-start.2 = ((bf16[64,16,512]{2,0,1:T(8,128)(2,1)}), bf16[64,16,512]{2,0,1:T(8,128)(2,1)S(1)}, u32[]{:S(2)}, u32[]{:S(2)}) async-start(bf16[64,16,512]{2,0,1:T(8,128)(2,1)} %bitcast.11), calls=%async_computation.2 | async-start | bytes 2097152 | tf_op jit(solution)/shard_map/all_to_all | solution.py:102
  61.0 38.6 %all-to-all-start.3 = ((bf16[64,16,512]{2,0,1:T(8,128)(2,1)}), bf16[64,16,512]{2,0,1:T(8,128)(2,1)S(1)}, u32[]{:S(2)}, u32[]{:S(2)}) async-start(bf16[64,16,512]{2,0,1:T(8,128)(2,1)} %bitcast.13), calls=%async_computation.3 | async-start | bytes 2097152 | tf_op jit(solution)/shard_map/all_to_all | solution.py:103
  67.1 27.8 %collective-permute-start = (bf16[2,1024,128]{2,1,0:T(8,128)(2,1)}, bf16[2,1024,128]{2,1,0:T(8,128)(2,1)S(1)}, u32[]{:S(2)}, u32[]{:S(2)}) collective-permute-start(bf16[2,1024,128]{2,1,0:T(8,128)(2,1)} %pad_maximum_fusion), channel_id=1, source_target_pairs={{0,1},{1,2},{2,3},{3,4},{4,5},{5,6},{6,7},{7,8},{8,9},{9,10},{10,1... | collective-permute-start | bytes 1572872 | tf_op jit(solution)/shard_map/ppermute | solution.py:38
  210.5 12.0 %collective-permute-start.1 = (bf16[2,1024,128]{2,1,0:T(8,128)(2,1)S(1)}, bf16[2,1024,128]{2,1,0:T(8,128)(2,1)S(1)}, u32[]{:S(2)}, u32[]{:S(2)}) collective-permute-start(bf16[2,1024,128]{2,1,0:T(8,128)(2,1)S(1)} %pad_maximum_fusion.3), channel_id=1, source_target_pairs={{1,0},{2,1},{3,2},{4,3},{5,4},{6,5},{7,6},{8,7},{9,8},{10,9},{11,1... | collective-permute-start | bytes 1572872 | tf_op jit(solution)/shard_map/ppermute | solution.py:38
  224.7 11.9 %all-to-all-start.6 = ((bf16[64,16,128]{2,0,1:T(8,128)(2,1)}), bf16[64,16,128]{2,0,1:T(8,128)(2,1)S(1)}, u32[]{:S(2)}, u32[]{:S(2)}) async-start(bf16[64,16,128]{2,0,1:T(8,128)(2,1)} %copy.109), calls=%async_computation.6 | async-start | bytes 524288 | tf_op jit(solution)/shard_map/all_to_all | solution.py:170
  236.6 32.3 %all-to-all-start.5 = ((bf16[64,16,512]{2,0,1:T(8,128)(2,1)}), bf16[64,16,512]{2,0,1:T(8,128)(2,1)S(1)}, u32[]{:S(2)}, u32[]{:S(2)}) async-start(bf16[64,16,512]{2,0,1:T(8,128)(2,1)} %copy.107), calls=%async_computation.5 | async-start | bytes 2097152 | tf_op jit(solution)/shard_map/all_to_all | solution.py:169
  245.1 4.1 %collective-permute-start.2 = (bf16[64,1,128]{2,0,1:T(8,128)(2,1)S(1)}, bf16[64,1,128]{2,0,1:T(8,128)(2,1)S(1)}, u32[]{:S(2)}, u32[]{:S(2)}) collective-permute-start(bf16[64,1,128]{2,0,1:T(8,128)(2,1)S(1)} %bitcast.302), channel_id=1, source_target_pairs={{0,1},{1,0},{2,3},{3,2},{4,5},{5,4},{6,7},{7,6},{8,9},{9,8},{10,11... | collective-permute-start | bytes 49160 | tf_op jit(solution)/shard_map/ppermute | solution.py:30
  245.6 3.9 %collective-permute-start.3 = (bf16[64,1,128]{2,0,1:T(8,128)(2,1)S(1)}, bf16[64,1,128]{2,0,1:T(8,128)(2,1)S(1)}, u32[]{:S(2)}, u32[]{:S(2)}) collective-permute-start(bf16[64,1,128]{2,0,1:T(8,128)(2,1)S(1)} %bitcast.301), channel_id=1, source_target_pairs={{0,2},{1,3},{2,0},{3,1},{4,6},{5,7},{6,4},{7,5},{8,10},{9,11},{10,... | collective-permute-start | bytes 49160 | tf_op jit(solution)/shard_map/ppermute | solution.py:30
  245.9 6.1 %collective-permute-start.4 = (bf16[64,1,128]{2,0,1:T(8,128)(2,1)S(1)}, bf16[64,1,128]{2,0,1:T(8,128)(2,1)S(1)}, u32[]{:S(2)}, u32[]{:S(2)}) collective-permute-start(bf16[64,1,128]{2,0,1:T(8,128)(2,1)S(1)} %bitcast.300), channel_id=1, source_target_pairs={{0,3},{1,2},{2,1},{3,0},{4,7},{5,6},{6,5},{7,4},{8,11},{9,10},{10,... | collective-permute-start | bytes 49160 | tf_op jit(solution)/shard_map/ppermute | solution.py:30
  247.4 13.4 %collective-permute-start.5 = (bf16[64,1,128]{2,0,1:T(8,128)(2,1)S(1)}, bf16[64,1,128]{2,0,1:T(8,128)(2,1)S(1)}, u32[]{:S(2)}, u32[]{:S(2)}) collective-permute-start(bf16[64,1,128]{2,0,1:T(8,128)(2,1)S(1)} %bitcast.299), channel_id=1, source_target_pairs={{0,4},{1,5},{2,6},{3,7},{4,0},{5,1},{6,2},{7,3},{8,12},{9,13},{10,... | collective-permute-start | bytes 49160 | tf_op jit(solution)/shard_map/ppermute | solution.py:30
  247.7 15.6 %collective-permute-start.6 = (bf16[64,1,128]{2,0,1:T(8,128)(2,1)S(1)}, bf16[64,1,128]{2,0,1:T(8,128)(2,1)S(1)}, u32[]{:S(2)}, u32[]{:S(2)}) collective-permute-start(bf16[64,1,128]{2,0,1:T(8,128)(2,1)S(1)} %bitcast.298), channel_id=1, source_target_pairs={{0,5},{1,4},{2,7},{3,6},{4,1},{5,0},{6,3},{7,2},{8,13},{9,12},{10,... | collective-permute-start | bytes 49160 | tf_op jit(solution)/shard_map/ppermute | solution.py:30
  249.3 14.8 %collective-permute-start.7 = (bf16[64,1,128]{2,0,1:T(8,128)(2,1)S(1)}, bf16[64,1,128]{2,0,1:T(8,128)(2,1)S(1)}, u32[]{:S(2)}, u32[]{:S(2)}) collective-permute-start(bf16[64,1,128]{2,0,1:T(8,128)(2,1)S(1)} %bitcast.297), channel_id=1, source_target_pairs={{0,6},{1,7},{2,4},{3,5},{4,2},{5,3},{6,0},{7,1},{8,14},{9,15},{10,... | collective-permute-start | bytes 49160 | tf_op jit(solution)/shard_map/ppermute | solution.py:30
  249.5 23.8 %collective-permute-start.8 = (bf16[64,1,128]{2,0,1:T(8,128)(2,1)S(1)}, bf16[64,1,128]{2,0,1:T(8,128)(2,1)S(1)}, u32[]{:S(2)}, u32[]{:S(2)}) collective-permute-start(bf16[64,1,128]{2,0,1:T(8,128)(2,1)S(1)} %bitcast.296), channel_id=1, source_target_pairs={{0,7},{1,6},{2,5},{3,4},{4,3},{5,2},{6,1},{7,0},{8,15},{9,14},{10,... | collective-permute-start | bytes 49160 | tf_op jit(solution)/shard_map/ppermute | solution.py:30
  252.0 22.5 %collective-permute-start.9 = (bf16[64,1,128]{2,0,1:T(8,128)(2,1)S(1)}, bf16[64,1,128]{2,0,1:T(8,128)(2,1)S(1)}, u32[]{:S(2)}, u32[]{:S(2)}) collective-permute-start(bf16[64,1,128]{2,0,1:T(8,128)(2,1)S(1)} %bitcast.295), channel_id=1, source_target_pairs={{0,8},{1,9},{2,10},{3,11},{4,12},{5,13},{6,14},{7,15},{8,0},{9,1},... | collective-permute-start | bytes 49160 | tf_op jit(solution)/shard_map/ppermute | solution.py:30
  260.8 14.5 %collective-permute-start.10 = (bf16[64,1,128]{2,0,1:T(8,128)(2,1)S(1)}, bf16[64,1,128]{2,0,1:T(8,128)(2,1)S(1)}, u32[]{:S(2)}, u32[]{:S(2)}) collective-permute-start(bf16[64,1,128]{2,0,1:T(8,128)(2,1)S(1)} %bitcast.294), channel_id=1, source_target_pairs={{0,9},{1,8},{2,11},{3,10},{4,13},{5,12},{6,15},{7,14},{8,1},{9,0},... | collective-permute-start | bytes 49160 | tf_op jit(solution)/shard_map/ppermute | solution.py:30
  263.3 13.2 %collective-permute-start.11 = (bf16[64,1,128]{2,0,1:T(8,128)(2,1)S(1)}, bf16[64,1,128]{2,0,1:T(8,128)(2,1)S(1)}, u32[]{:S(2)}, u32[]{:S(2)}) collective-permute-start(bf16[64,1,128]{2,0,1:T(8,128)(2,1)S(1)} %bitcast.293), channel_id=1, source_target_pairs={{0,10},{1,11},{2,8},{3,9},{4,14},{5,15},{6,12},{7,13},{8,2},{9,3},... | collective-permute-start | bytes 49160 | tf_op jit(solution)/shard_map/ppermute | solution.py:30
  264.1 13.7 %collective-permute-start.12 = (bf16[64,1,128]{2,0,1:T(8,128)(2,1)S(1)}, bf16[64,1,128]{2,0,1:T(8,128)(2,1)S(1)}, u32[]{:S(2)}, u32[]{:S(2)}) collective-permute-start(bf16[64,1,128]{2,0,1:T(8,128)(2,1)S(1)} %bitcast.292), channel_id=1, source_target_pairs={{0,11},{1,10},{2,9},{3,8},{4,15},{5,14},{6,13},{7,12},{8,3},{9,2},... | collective-permute-start | bytes 49160 | tf_op jit(solution)/shard_map/ppermute | solution.py:30
  268.9 37.5 %all-to-all-start.4 = ((bf16[64,16,512]{2,0,1:T(8,128)(2,1)}), bf16[64,16,512]{2,0,1:T(8,128)(2,1)S(1)}, u32[]{:S(2)}, u32[]{:S(2)}) async-start(bf16[64,16,512]{2,0,1:T(8,128)(2,1)} %copy.104), calls=%async_computation.4 | async-start | bytes 2097152 | tf_op jit(solution)/shard_map/all_to_all | solution.py:168
  273.2 26.1 %collective-permute-start.13 = (bf16[64,1,128]{2,0,1:T(8,128)(2,1)S(1)}, bf16[64,1,128]{2,0,1:T(8,128)(2,1)S(1)}, u32[]{:S(2)}, u32[]{:S(2)}) collective-permute-start(bf16[64,1,128]{2,0,1:T(8,128)(2,1)S(1)} %bitcast.291), channel_id=1, source_target_pairs={{0,12},{1,13},{2,14},{3,15},{4,8},{5,9},{6,10},{7,11},{8,4},{9,5},... | collective-permute-start | bytes 49160 | tf_op jit(solution)/shard_map/ppermute | solution.py:30
  274.5 26.4 %collective-permute-start.14 = (bf16[64,1,128]{2,0,1:T(8,128)(2,1)S(1)}, bf16[64,1,128]{2,0,1:T(8,128)(2,1)S(1)}, u32[]{:S(2)}, u32[]{:S(2)}) collective-permute-start(bf16[64,1,128]{2,0,1:T(8,128)(2,1)S(1)} %bitcast.290), channel_id=1, source_target_pairs={{0,13},{1,12},{2,15},{3,14},{4,9},{5,8},{6,11},{7,10},{8,5},{9,4},... | collective-permute-start | bytes 49160 | tf_op jit(solution)/shard_map/ppermute | solution.py:30
  275.3 25.6 %collective-permute-start.15 = (bf16[64,1,128]{2,0,1:T(8,128)(2,1)S(1)}, bf16[64,1,128]{2,0,1:T(8,128)(2,1)S(1)}, u32[]{:S(2)}, u32[]{:S(2)}) collective-permute-start(bf16[64,1,128]{2,0,1:T(8,128)(2,1)S(1)} %bitcast.289), channel_id=1, source_target_pairs={{0,14},{1,15},{2,12},{3,13},{4,10},{5,11},{6,8},{7,9},{8,6},{9,7},... | collective-permute-start | bytes 49160 | tf_op jit(solution)/shard_map/ppermute | solution.py:30
  276.5 24.5 %collective-permute-start.16 = (bf16[64,1,128]{2,0,1:T(8,128)(2,1)S(1)}, bf16[64,1,128]{2,0,1:T(8,128)(2,1)S(1)}, u32[]{:S(2)}, u32[]{:S(2)}) collective-permute-start(bf16[64,1,128]{2,0,1:T(8,128)(2,1)S(1)} %bitcast.288), channel_id=1, source_target_pairs={{0,15},{1,14},{2,13},{3,12},{4,11},{5,10},{6,9},{7,8},{8,7},{9,6},... | collective-permute-start | bytes 49160 | tf_op jit(solution)/shard_map/ppermute | solution.py:30
  (8 other events, 168.6 us)
